TPU v7x, 32 devices: a whole 2x2x4 slice. The times are simulated.
32 devices in a mesh: expert: 4 (over x, core), group: 8 (over z, y).
Axes of the slice: x: 2, y: 2, z: 4, core: 2. Of those that a mesh axis runs over, the one named last changes fastest.
Arguments:
- tokens: bfloat16 [16384, 2048], P(('expert', 'group')), may hold values from -6 to 6
- routing: int32 [16384, 8], P(('expert', 'group')), may hold values from 0 to 31, as said below
- mixing: float32 [16384, 8], P(('expert', 'group')), may hold values from 0.1 to 1
- visited: int32 [4], replicated, may hold values from 0 to 31, as said below
- gate_matrix: bfloat16 [32, 2048, 768], P('expert', 'group'), may hold values from -0.125 to 0.125
- up_matrix: bfloat16 [32, 2048, 768], P('expert', 'group'), may hold values from -0.125 to 0.125
- down_matrix: bfloat16 [32, 768, 2048], P('expert', None, 'group'), may hold values from -0.21875 to 0.21875
Outputs:
- combined: bfloat16 [16384, 2048], P(('expert', 'group'))
Inputs may be any that keep to these rules, and one draw needn't show every extreme that they name: `routing`: each row names 8 different experts. In the rows of one device, each expert of visited is named by at least half of 80 (rounded up) and at most 80 rows, and for each visited expert some device has exactly 80 such rows. `visited`: 4 different experts.
All inputs are finite; a program needn't handle non-finite values.
Results may differ from a plain program's by a relative error of at most 0.0049.
Values may be sent and summed in bfloat16 or wider, within the bound.
No kernel may reach another device: no remote copies, remote signals or barrier semaphores. Data moves between devices by JAX's collectives and lax.ppermute only.
A program may use at most 128 MiB of HBM per device.

v0:
```python
import jax
import jax.numpy as jnp
from jax import lax
from jax.sharding import PartitionSpec as P

VISITS = 4
CAP = 80


def from_root(value, axis, source):
    kept = jnp.where(lax.axis_index(axis) == source, value, 0).astype(value.dtype)
    return lax.psum(kept, axis)


def select_rows(routing, mixing, target, capacity):
    hit = routing == target
    member = jnp.any(hit, axis=1)
    share = jnp.sum(jnp.where(hit, mixing, jnp.zeros_like(mixing)), axis=1)
    place = jnp.cumsum(member.astype(jnp.int32)) - 1
    slots = jnp.arange(capacity, dtype=jnp.int32)
    table = member[:, None] & (place[:, None] == slots[None, :])
    indices = jnp.arange(routing.shape[0], dtype=jnp.int32)
    rows = jnp.sum(jnp.where(table, indices[:, None], 0), axis=0)
    filled = jnp.any(table, axis=0)
    scales = jnp.where(filled, share[rows], jnp.zeros_like(share[rows]))
    return (rows, scales)


def body(tokens, routing, mixing, visited, gate_matrix, up_matrix, down_matrix):
    held = gate_matrix.shape[0]
    combined = jnp.zeros(tokens.shape, jnp.float32)
    for number in range(VISITS):
        target = visited[number]
        rows, scales = select_rows(routing, mixing, target, CAP)
        picked = tokens[rows]
        owner = target // held
        local = target % held
        slices = (
            lax.dynamic_index_in_dim(gate_matrix, local, 0, keepdims=False),
            lax.dynamic_index_in_dim(up_matrix, local, 0, keepdims=False),
            lax.dynamic_index_in_dim(down_matrix, local, 0, keepdims=False),
        )
        gate_slice, up_slice, down_slice = (
            from_root(slices[0], "expert", owner),
            from_root(slices[1], "expert", owner),
            from_root(slices[2], "expert", owner),
        )
        empty = jnp.zeros((CAP, gate_slice.shape[1]), jnp.float32)

        def add_both(totals, pieces, start, picked=picked):
            return (
                jnp.dot(picked, pieces[0], preferred_element_type=jnp.float32),
                jnp.dot(picked, pieces[1], preferred_element_type=jnp.float32),
            )

        gate, up = add_both(
            (empty, empty),
            (
                lax.all_gather(gate_slice, "group", axis=0, tiled=True),
                lax.all_gather(up_slice, "group", axis=0, tiled=True),
            ),
            jnp.int32(0),
        )
        hidden = (jax.nn.silu(gate) * up).astype(jnp.bfloat16)

        def partial_columns(piece, start, down_slice=down_slice):
            return jnp.dot(piece, down_slice, preferred_element_type=jnp.float32)

        column_parts = partial_columns(
            lax.all_gather(hidden, "group", axis=0, tiled=True), jnp.int32(0)
        )
        expert_output = lax.all_to_all(
            column_parts, "group", split_axis=0, concat_axis=1, tiled=True
        )
        combined = combined.at[rows].add(scales[:, None] * expert_output)
    return combined.astype(jnp.bfloat16)


def solution(mesh):
    placed = (
        P(("expert", "group"), None),
        P(("expert", "group"), None),
        P(("expert", "group"), None),
        P(),
        P("expert", "group", None),
        P("expert", "group", None),
        P("expert", None, "group"),
    )
    return jax.shard_map(
        body, mesh=mesh, in_specs=placed, out_specs=P(("expert", "group"), None), check_vma=False
    )
```

profile of v0, /device:TPU:0, one launch (start us, length us, event | category | flops | bytes accessed | tf_op | source)
XLA Modules:
  0.0 753.0 jit_solution(4360539912461578354)
XLA Ops:
  6.5 1.5 fusion.32
  18.0 2.7 select_bitcast_fusion
  20.7 3.0 select_bitcast_fusion.1
  23.8 97.0 %all-reduce.3.cloned.1.call-done = (bf16[256,768]{1,0:T(8,128)(2,1)}, bf16[256,768]{1,0:T(8,128)(2,1)}, bf16[768,256]{1,0:T(8,128)(2,1)}, bf16[256,768]{1,0:T(8,...) async-done(((bf16[256,768]{1,0:T(8,128)(2,1)}, ...) | async-done | bytes 4718608 | tf_op jit(solution)/shard_map/psum | solution.py:12
  120.9 0.7 all-gather.15.cloned.1.call-update
  121.7 0.5 all-gather.9.cloned.1.call-update
  122.2 0.5 all-gather.11.cloned.1.call-update
  122.8 0.5 all-gather.17.cloned.1.call-update
  123.4 0.7 all-gather.19.cloned.1.call-update
  124.1 0.7 all-gather.21.cloned.1.call-update
  124.9 1.9 fusion.30
  126.8 0.6 select_reduce_fusion.4
  127.5 0.3 reduce-window.34
  127.9 0.3 reduce-window.36
  128.3 0.3 reduce-window.50
  128.7 0.3 reduce-window.48
  129.2 0.2 slice_reduce_fusion.2
  129.8 0.1 select_reduce_fusion.3
  130.1 0.8 gather_fusion.3
  130.9 0.8 gather_fusion.1
  131.8 0.2 select_reduce_fusion
  131.9 0.8 gather_fusion.5
  132.8 0.8 gather_fusion.7
  133.7 49.8 %all-gather.13.cloned.1.call-done = bf16[2048,768]{1,0:T(8,128)(2,1)} async-done(((bf16[256,768]{1,0:T(8,128)(2,1)}), bf16[2048,768]{1,0:T(8,128)(2,1)}) %all-gather.13.cloned.1.call-update) | async-done | bytes 3145744 | tf_op jit(solution)/shard_map/all_gather | solution.py:59
  183.5 2.5 fusion.35
  186.0 58.4 %all-gather.15.cloned.1.call-done = bf16[2048,768]{1,0:T(8,128)(2,1)} async-done(((bf16[256,768]{1,0:T(8,128)(2,1)}), bf16[2048,768]{1,0:T(8,128)(2,1)}) %all-gather.15.cloned.1.call-update) | async-done | bytes 3145744 | tf_op jit(solution)/shard_map/all_gather | solution.py:60
  244.4 2.5 fusion.3
  246.9 34.9 %all_gather.41 = bf16[640,768]{1,0:T(8,128)(2,1)S(1)} all-gather(bf16[80,768]{1,0:T(8,128)(2,1)S(1)} %fusion.3), channel_id=1, replica_groups=mesh['expert'=4,'group'=8] {'group'}, dimensions={0}, use_global_device_ids=true | all-gather | bytes 1105920 | tf_op jit(solution)/shard_map/all_gather | solution.py:70
  281.8 1.3 fusion.36
  283.1 3.5 all-to-all-start.1
  286.6 37.5 %all-gather.9.cloned.1.call-done = bf16[2048,768]{1,0:T(8,128)(2,1)} async-done(((bf16[256,768]{1,0:T(8,128)(2,1)}), bf16[2048,768]{1,0:T(8,128)(2,1)}) %all-gather.9.cloned.1.call-update) | async-done | bytes 3145744 | tf_op jit(solution)/shard_map/all_gather | solution.py:59
  324.2 2.5 fusion.33
  326.7 58.5 %all-gather.11.cloned.1.call-done = bf16[2048,768]{1,0:T(8,128)(2,1)} async-done(((bf16[256,768]{1,0:T(8,128)(2,1)}), bf16[2048,768]{1,0:T(8,128)(2,1)}) %all-gather.11.cloned.1.call-update) | async-done | bytes 3145744 | tf_op jit(solution)/shard_map/all_gather | solution.py:60
  385.2 2.5 fusion.2
  387.8 34.9 %all_gather.38 = bf16[640,768]{1,0:T(8,128)(2,1)S(1)} all-gather(bf16[80,768]{1,0:T(8,128)(2,1)S(1)} %fusion.2), channel_id=1, replica_groups=mesh['expert'=4,'group'=8] {'group'}, dimensions={0}, use_global_device_ids=true | all-gather | bytes 1105920 | tf_op jit(solution)/shard_map/all_gather | solution.py:70
  422.7 1.3 fusion.34
  423.9 3.5 all-to-all-start
  427.5 37.6 %all-gather.17.cloned.1.call-done = bf16[2048,768]{1,0:T(8,128)(2,1)} async-done(((bf16[256,768]{1,0:T(8,128)(2,1)}), bf16[2048,768]{1,0:T(8,128)(2,1)}) %all-gather.17.cloned.1.call-update) | async-done | bytes 3145744 | tf_op jit(solution)/shard_map/all_gather | solution.py:59
  465.1 2.5 fusion.37
  467.6 58.7 %all-gather.19.cloned.1.call-done = bf16[2048,768]{1,0:T(8,128)(2,1)} async-done(((bf16[256,768]{1,0:T(8,128)(2,1)}), bf16[2048,768]{1,0:T(8,128)(2,1)}) %all-gather.19.cloned.1.call-update) | async-done | bytes 3145744 | tf_op jit(solution)/shard_map/all_gather | solution.py:60
  526.3 2.6 fusion.4
  528.9 34.9 %all_gather.44 = bf16[640,768]{1,0:T(8,128)(2,1)S(1)} all-gather(bf16[80,768]{1,0:T(8,128)(2,1)S(1)} %fusion.4), channel_id=1, replica_groups=mesh['expert'=4,'group'=8] {'group'}, dimensions={0}, use_global_device_ids=true | all-gather | bytes 1105920 | tf_op jit(solution)/shard_map/all_gather | solution.py:70
  563.8 1.3 fusion.38
  565.0 4.2 all-to-all-start.2
  569.2 37.3 %all-gather.21.cloned.1.call-done = bf16[2048,768]{1,0:T(8,128)(2,1)} async-done(((bf16[256,768]{1,0:T(8,128)(2,1)}), bf16[2048,768]{1,0:T(8,128)(2,1)}) %all-gather.21.cloned.1.call-update) | async-done | bytes 3145744 | tf_op jit(solution)/shard_map/all_gather | solution.py:59
  606.6 2.5 fusion.39
  609.1 58.7 %all-gather.23.cloned.1.call-done = bf16[2048,768]{1,0:T(8,128)(2,1)} async-done(((bf16[256,768]{1,0:T(8,128)(2,1)}), bf16[2048,768]{1,0:T(8,128)(2,1)}) %all-gather.23.cloned.1.call-update) | async-done | bytes 3145744 | tf_op jit(solution)/shard_map/all_gather | solution.py:60
  667.8 2.6 fusion.5
  670.4 32.8 %all_gather.47 = bf16[640,768]{1,0:T(8,128)(2,1)S(1)} all-gather(bf16[80,768]{1,0:T(8,128)(2,1)S(1)} %fusion.5), channel_id=1, replica_groups=mesh['expert'=4,'group'=8] {'group'}, dimensions={0}, use_global_device_ids=true | all-gather | bytes 1105920 | tf_op jit(solution)/shard_map/all_gather | solution.py:70
  703.1 1.3 fusion.40
  704.4 3.7 all-to-all-start.3
  708.3 1.3 gather_fusion
  709.5 1.3 gather_fusion.2
  710.8 1.3 gather_fusion.4
  712.1 1.3 gather_fusion.6
  713.8 1.1 copy.22
  714.9 4.6 all-to-all-done.3
  719.6 0.8 copy-done.2
  720.4 1.1 copy.23
  721.5 3.8 scatter_custom_fusion
  725.4 5.7 scatter_custom_fusion.1
  731.1 5.7 scatter_custom_fusion.2
  736.8 5.9 scatter_custom_fusion.3
  742.7 3.8 convert_element_type.69
  (72 shorter events, 2.2 us)
Async XLA Ops:
  6.5 123.6 %copy-start = (bf16[512,2048]{1,0:T(8,128)(2,1)S(1)}, bf16[512,2048]{1,0:T(8,128)(2,1)}, u32[]{:S(2)}) copy-start(bf16[512,2048]{1,0:T(8,128)(2,1)} %param.7) | copy-start | bytes 6291460
  6.5 114.3 %all-reduce.3.cloned.1.call-start = ((), (), s32[]{:S(2)}) async-start(), calls=%async_computation.12 | async-start | bytes 9437184 | tf_op jit(solution)/shard_map/psum | solution.py:12
  18.0 2.7 copy-start.3
  23.7 101.2 %copy-start.8 = (s32[512,8]{0,1:T(8,128)S(1)}, s32[512,8]{0,1:T(8,128)}, u32[]{:S(2)}) copy-start(s32[512,8]{0,1:T(8,128)} %param.8) | copy-start | bytes 49156
  23.7 103.1 %copy-start.9 = (f32[512,8]{0,1:T(8,128)S(1)}, f32[512,8]{0,1:T(8,128)}, u32[]{:S(2)}) copy-start(f32[512,8]{0,1:T(8,128)} %param.9) | copy-start | bytes 49156
  23.8 159.7 %all-gather.13.cloned.1.call-start = ((), (), s32[]{:S(2)}) async-start(), calls=%async_computation.6 | async-start | bytes 3538944 | tf_op jit(solution)/shard_map/all_gather | solution.py:59
  120.9 123.5 %all-gather.15.cloned.1.call-start = ((), (), s32[]{:S(2)}) async-start(), calls=%async_computation.7 | async-start | bytes 3538944 | tf_op jit(solution)/shard_map/all_gather | solution.py:60
  121.6 202.6 %all-gather.9.cloned.1.call-start = ((), (), s32[]{:S(2)}) async-start(), calls=%async_computation.4 | async-start | bytes 3538944 | tf_op jit(solution)/shard_map/all_gather | solution.py:59
  122.2 263.1 %all-gather.11.cloned.1.call-start = ((), (), s32[]{:S(2)}) async-start(), calls=%async_computation.5 | async-start | bytes 3538944 | tf_op jit(solution)/shard_map/all_gather | solution.py:60
  122.8 342.3 %all-gather.17.cloned.1.call-start = ((), (), s32[]{:S(2)}) async-start(), calls=%async_computation.8 | async-start | bytes 3538944 | tf_op jit(solution)/shard_map/all_gather | solution.py:59
  123.3 402.9 %all-gather.19.cloned.1.call-start = ((), (), s32[]{:S(2)}) async-start(), calls=%async_computation.9 | async-start | bytes 3538944 | tf_op jit(solution)/shard_map/all_gather | solution.py:60
  124.1 482.5 %all-gather.21.cloned.1.call-start = ((), (), s32[]{:S(2)}) async-start(), calls=%async_computation.10 | async-start | bytes 3538944 | tf_op jit(solution)/shard_map/all_gather | solution.py:59
  124.8 542.9 %all-gather.23.cloned.1.call-start = ((), (), s32[]{:S(2)}) async-start(), calls=%async_computation.11 | async-start | bytes 3538944 | tf_op jit(solution)/shard_map/all_gather | solution.py:60
  186.0 95.8 %copy-start.7 = (bf16[768,256]{1,0:T(8,128)(2,1)S(1)}, bf16[768,256]{1,0:T(8,128)(2,1)}, u32[]{:S(2)}) copy-start(bf16[768,256]{1,0:T(8,128)(2,1)} %get-tuple-element.14) | copy-start | bytes 1179652
  283.1 140.9 %all-to-all-start.1 = ((f32[8,80,256]{2,1,0:T(8,128)}), f32[8,80,256]{2,1,0:T(8,128)S(1)}, u32[]{:S(2)}, u32[]{:S(2)}) async-start(f32[8,80,256]{2,1,0:T(8,128)} %bitcast.108), calls=%async_computation.1 | async-start | bytes 1310720 | tf_op jit(solution)/shard_map/all_to_all | solution.py:72
  326.7 96.0 %copy-start.6 = (bf16[768,256]{1,0:T(8,128)(2,1)S(1)}, bf16[768,256]{1,0:T(8,128)(2,1)}, u32[]{:S(2)}) copy-start(bf16[768,256]{1,0:T(8,128)(2,1)} %get-tuple-element.11) | copy-start | bytes 1179652
  423.9 141.1 %all-to-all-start = ((f32[8,80,256]{2,1,0:T(8,128)}), f32[8,80,256]{2,1,0:T(8,128)S(1)}, u32[]{:S(2)}, u32[]{:S(2)}) async-start(f32[8,80,256]{2,1,0:T(8,128)} %bitcast.107), calls=%async_computation | async-start | bytes 1310720 | tf_op jit(solution)/shard_map/all_to_all | solution.py:72
  526.3 37.5 %copy-start.5 = (bf16[768,256]{1,0:T(8,128)(2,1)S(1)}, bf16[768,256]{1,0:T(8,128)(2,1)}, u32[]{:S(2)}) copy-start(bf16[768,256]{1,0:T(8,128)(2,1)} %get-tuple-element.17) | copy-start | bytes 1179652
  565.0 139.4 %all-to-all-start.2 = ((f32[8,80,256]{2,1,0:T(8,128)}), f32[8,80,256]{2,1,0:T(8,128)}, u32[]{:S(2)}, u32[]{:S(2)}) async-start(f32[8,80,256]{2,1,0:T(8,128)} %bitcast.106), calls=%async_computation.2 | async-start | bytes 1310720 | tf_op jit(solution)/shard_map/all_to_all | solution.py:72
  667.8 35.3 %copy-start.4 = (bf16[768,256]{1,0:T(8,128)(2,1)S(1)}, bf16[768,256]{1,0:T(8,128)(2,1)}, u32[]{:S(2)}) copy-start(bf16[768,256]{1,0:T(8,128)(2,1)} %get-tuple-element.20) | copy-start | bytes 1179652
  704.4 15.2 %all-to-all-start.3 = ((f32[8,80,256]{2,1,0:T(8,128)}), f32[8,80,256]{2,1,0:T(8,128)S(1)}, u32[]{:S(2)}, u32[]{:S(2)}) async-start(f32[8,80,256]{2,1,0:T(8,128)} %bitcast.38), calls=%async_computation.3 | async-start | bytes 1310720 | tf_op jit(solution)/shard_map/all_to_all | solution.py:72
  719.6 0.8 copy-start.2
  736.8 9.7 %copy-start.1 = (bf16[512,2048]{1,0:T(8,128)(2,1)S(1)}, bf16[512,2048]{1,0:T(8,128)(2,1)}, u32[]{:S(2)}) copy-start(bf16[512,2048]{1,0:T(8,128)(2,1)} %param.7) | copy-start | bytes 6291460
Sparse Core Ops, SparseCore 0:
  23.9 96.9 all-reduce.2
  123.0 60.3 all-gather.12
  185.7 58.6 all-gather.14
  246.4 77.7 all-gather.8
  326.2 58.9 all-gather.10
  387.3 77.7 all-gather.16
  467.2 58.9 all-gather.18
  528.5 78.0 all-gather.20
  608.8 58.9 all-gather.22
where the time goes:
time: 754 us; the launch traced here: 753 us
  waiting for transfers between devices  502 us (67%)
  blocking collectives  137 us (18%)
  other arithmetic  35.9 us (5%)
  matrix products  25.4 us (3%)
  between operations  23.4 us (3%)
  starting transfers between devices  15.3 us (2%)
  local copies, waits for them, and re-layouts  13.7 us (2%)
    all_gather x4, waiting for transfers between devices, body(): lax.all_gather(up_slice, 'group', axis=0, tiled=True)  234 us
    all_gather x4, waiting for transfers between devices, body(): lax.all_gather(gate_slice, 'group', axis=0, tiled=True)  162 us
    all_gather x4, blocking collectives, body(): lax.all_gather(hidden, 'group', axis=0, tiled=True)  137 us
    psum x1, waiting for transfers between devices, from_root(): return lax.psum(kept, axis)  97 us
    scatter-add x4, other arithmetic, body(): combined = combined.at[rows].add(scales[:, None] * expert_output)  21.1 us
  transfers between devices with their start and end apart: 13, of which 10 were waited for; matrix products, arithmetic and copies ran while one was open for 5% of the time, Pallas kernels for 0%

commit v1 on v0

--- a/solution.py
+++ b/solution.py
@@ -9,7 +9,12 @@
 
 def from_root(value, axis, source):
     kept = jnp.where(lax.axis_index(axis) == source, value, 0).astype(value.dtype)
-    return lax.psum(kept, axis)
+
+    def meshes_solve(values):
+        t1 = jnp.sum(lax.all_gather(values, axis_name=axis), axis=0)
+        return t1
+
+    return meshes_solve(kept)
 
 
 def select_rows(routing, mixing, target, capacity):

time: 754 us -> 909 us (1.21)
  waiting for transfers between devices: 502 us -> 624 us
  other arithmetic: 35.9 us -> 66.4 us
    all_gather x0 -> x12, waiting for transfers between devices: none -> 208 us  [meshes_solve(): t1 = jnp.sum(lax.all_gather(values, axis_name=axis), axis=0)]
    psum x1 -> x0, waiting for transfers between devices: 97 us -> none  [from_root(): return lax.psum(kept, axis)]
    reduce_sum x0 -> x12, other arithmetic: none -> 28.6 us  [meshes_solve(): t1 = jnp.sum(lax.all_gather(values, axis_name=axis), axis=0)]
    all_gather x4, waiting for transfers between devices: 162 us -> 173 us  [body(): lax.all_gather(gate_slice, 'group', axis=0, tiled=True)]
  transfers between devices with their start and end apart: 13 -> 24, of which waited for: 10 -> 21; matrix products, arithmetic and copies ran while one was open for 5% -> 8% of each run, Pallas kernels for 0% -> 0%
where the time goes in v1:
time: 909 us; the launch traced here: 908 us
  waiting for transfers between devices  624 us (69%)
  blocking collectives  137 us (15%)
  other arithmetic  66.4 us (7%)
  matrix products  25.3 us (3%)
  between operations  24 us (3%)
  starting transfers between devices  15.8 us (2%)
  local copies, waits for them, and re-layouts  14.6 us (2%)
    all_gather x4, waiting for transfers between devices, body(): lax.all_gather(up_slice, 'group', axis=0, tiled=True)  234 us
    all_gather x12, waiting for transfers between devices, meshes_solve(): t1 = jnp.sum(lax.all_gather(values, axis_name=axis), axis=0)  208 us
    all_gather x4, waiting for transfers between devices, body(): lax.all_gather(gate_slice, 'group', axis=0, tiled=True)  173 us
    all_gather x4, blocking collectives, body(): lax.all_gather(hidden, 'group', axis=0, tiled=True)  137 us
    reduce_sum x12, other arithmetic, meshes_solve(): t1 = jnp.sum(lax.all_gather(values, axis_name=axis), axis=0)  28.6 us
    scatter-add x4, other arithmetic, body(): combined = combined.at[rows].add(scales[:, None] * expert_output)  21.1 us
  transfers between devices with their start and end apart: 24, of which 21 were waited for; matrix products, arithmetic and copies ran while one was open for 8% of the time, Pallas kernels for 0%

profile of v1, /device:TPU:0, one launch (start us, length us, event | category | flops | bytes accessed | tf_op | source)
XLA Modules:
  0.0 907.6 jit_solution(16596525335230926501)
XLA Ops:
  6.5 1.5 fusion.40
  18.0 2.5 dynamic-slice_select_fusion.2
  20.6 2.5 dynamic-slice_select_fusion.1
  27.2 2.6 dynamic-slice_select_fusion
  31.7 11.4 %all-gather.21.cloned.1.call-done = bf16[4,256,768]{2,1,0:T(8,128)(2,1)} async-done(((bf16[1,256,768]{2,1,0:T(8,128)(2,1)}), bf16[4,256,768]{2,1,0:T(8,128)(2,1)}) %all-gather.21.cloned.1.call-update) | async-done | bytes 1572880 | tf_op jit(solution)/shard_map/all_gather | solution.py:14
  43.1 2.5 reduce_sum.227
  45.7 18.7 %all-gather.25.cloned.1.call-done = bf16[4,256,768]{2,1,0:T(8,128)(2,1)} async-done(((bf16[1,256,768]{2,1,0:T(8,128)(2,1)}), bf16[4,256,768]{2,1,0:T(8,128)(2,1)}) %all-gather.25.cloned.1.call-update) | async-done | bytes 1572880 | tf_op jit(solution)/shard_map/all_gather | solution.py:14
  64.3 2.5 reduce_sum.228
  66.9 18.7 %all-gather.31.cloned.1.call-done = bf16[4,256,768]{2,1,0:T(8,128)(2,1)} async-done(((bf16[1,256,768]{2,1,0:T(8,128)(2,1)}), bf16[4,256,768]{2,1,0:T(8,128)(2,1)}) %all-gather.31.cloned.1.call-update) | async-done | bytes 1572880 | tf_op jit(solution)/shard_map/all_gather | solution.py:14
  85.6 2.5 reduce_sum.233
  88.1 18.5 %all-gather.35.cloned.1.call-done = bf16[4,256,768]{2,1,0:T(8,128)(2,1)} async-done(((bf16[1,256,768]{2,1,0:T(8,128)(2,1)}), bf16[4,256,768]{2,1,0:T(8,128)(2,1)}) %all-gather.35.cloned.1.call-update) | async-done | bytes 1572880 | tf_op jit(solution)/shard_map/all_gather | solution.py:14
  106.6 2.5 reduce_sum.234
  109.2 18.5 %all-gather.41.cloned.1.call-done = bf16[4,256,768]{2,1,0:T(8,128)(2,1)} async-done(((bf16[1,256,768]{2,1,0:T(8,128)(2,1)}), bf16[4,256,768]{2,1,0:T(8,128)(2,1)}) %all-gather.41.cloned.1.call-update) | async-done | bytes 1572880 | tf_op jit(solution)/shard_map/all_gather | solution.py:14
  127.7 2.5 reduce_sum.239
  130.3 18.5 %all-gather.45.cloned.1.call-done = bf16[4,256,768]{2,1,0:T(8,128)(2,1)} async-done(((bf16[1,256,768]{2,1,0:T(8,128)(2,1)}), bf16[4,256,768]{2,1,0:T(8,128)(2,1)}) %all-gather.45.cloned.1.call-update) | async-done | bytes 1572880 | tf_op jit(solution)/shard_map/all_gather | solution.py:14
  148.8 2.5 reduce_sum.240
  151.4 18.7 %all-gather.51.cloned.1.call-done = bf16[4,256,768]{2,1,0:T(8,128)(2,1)} async-done(((bf16[1,256,768]{2,1,0:T(8,128)(2,1)}), bf16[4,256,768]{2,1,0:T(8,128)(2,1)}) %all-gather.51.cloned.1.call-update) | async-done | bytes 1572880 | tf_op jit(solution)/shard_map/all_gather | solution.py:14
  170.0 2.5 reduce_sum.245
  172.6 1.9 fusion.38
  177.7 13.5 %all-gather.55.cloned.1.call-done = bf16[4,256,768]{2,1,0:T(8,128)(2,1)} async-done(((bf16[1,256,768]{2,1,0:T(8,128)(2,1)}), bf16[4,256,768]{2,1,0:T(8,128)(2,1)}) %all-gather.55.cloned.1.call-update) | async-done | bytes 1572880 | tf_op jit(solution)/shard_map/all_gather | solution.py:14
  191.2 2.5 reduce_sum.246
  197.4 15.1 %all-gather.29.cloned.1.call-done = bf16[4,768,256]{2,1,0:T(8,128)(2,1)} async-done(((bf16[1,768,256]{2,1,0:T(8,128)(2,1)}), bf16[4,768,256]{2,1,0:T(8,128)(2,1)}) %all-gather.29.cloned.1.call-update) | async-done | bytes 1572880 | tf_op jit(solution)/shard_map/all_gather | solution.py:14
  212.5 1.8 reduce_sum.229
  214.4 19.2 %all-gather.39.cloned.1.call-done = bf16[4,768,256]{2,1,0:T(8,128)(2,1)} async-done(((bf16[1,768,256]{2,1,0:T(8,128)(2,1)}), bf16[4,768,256]{2,1,0:T(8,128)(2,1)}) %all-gather.39.cloned.1.call-update) | async-done | bytes 1572880 | tf_op jit(solution)/shard_map/all_gather | solution.py:14
  233.6 2.5 reduce_sum.235
  236.1 18.7 %all-gather.49.cloned.1.call-done = bf16[4,768,256]{2,1,0:T(8,128)(2,1)} async-done(((bf16[1,768,256]{2,1,0:T(8,128)(2,1)}), bf16[4,768,256]{2,1,0:T(8,128)(2,1)}) %all-gather.49.cloned.1.call-update) | async-done | bytes 1572880 | tf_op jit(solution)/shard_map/all_gather | solution.py:14
  254.8 2.5 reduce_sum.241
  257.3 18.6 %all-gather.59.cloned.1.call-done = bf16[4,768,256]{2,1,0:T(8,128)(2,1)} async-done(((bf16[1,768,256]{2,1,0:T(8,128)(2,1)}), bf16[4,768,256]{2,1,0:T(8,128)(2,1)}) %all-gather.59.cloned.1.call-update) | async-done | bytes 1572880 | tf_op jit(solution)/shard_map/all_gather | solution.py:14
  275.9 1.8 reduce_sum.247
  277.7 60.4 %all-gather.23.cloned.1.call-done = bf16[2048,768]{1,0:T(8,128)(2,1)} async-done(((bf16[256,768]{1,0:T(8,128)(2,1)}), bf16[2048,768]{1,0:T(8,128)(2,1)}) %all-gather.23.cloned.1.call-update) | async-done | bytes 3145744 | tf_op jit(solution)/shard_map/all_gather | solution.py:64
  338.1 2.5 fusion.41
  340.7 58.2 %all-gather.27.cloned.1.call-done = bf16[2048,768]{1,0:T(8,128)(2,1)} async-done(((bf16[256,768]{1,0:T(8,128)(2,1)}), bf16[2048,768]{1,0:T(8,128)(2,1)}) %all-gather.27.cloned.1.call-update) | async-done | bytes 3145744 | tf_op jit(solution)/shard_map/all_gather | solution.py:65
  398.9 2.5 fusion.2
  401.4 34.9 %all_gather.88 = bf16[640,768]{1,0:T(8,128)(2,1)S(1)} all-gather(bf16[80,768]{1,0:T(8,128)(2,1)S(1)} %fusion.2), channel_id=1, replica_groups=mesh['expert'=4,'group'=8] {'group'}, dimensions={0}, use_global_device_ids=true | all-gather | bytes 1105920 | tf_op jit(solution)/shard_map/all_gather | solution.py:75
  437.6 3.5 all-to-all-start
  441.1 37.6 %all-gather.33.cloned.1.call-done = bf16[2048,768]{1,0:T(8,128)(2,1)} async-done(((bf16[256,768]{1,0:T(8,128)(2,1)}), bf16[2048,768]{1,0:T(8,128)(2,1)}) %all-gather.33.cloned.1.call-update) | async-done | bytes 3145744 | tf_op jit(solution)/shard_map/all_gather | solution.py:64
  478.7 2.5 fusion.42
  481.3 58.5 %all-gather.37.cloned.1.call-done = bf16[2048,768]{1,0:T(8,128)(2,1)} async-done(((bf16[256,768]{1,0:T(8,128)(2,1)}), bf16[2048,768]{1,0:T(8,128)(2,1)}) %all-gather.37.cloned.1.call-update) | async-done | bytes 3145744 | tf_op jit(solution)/shard_map/all_gather | solution.py:65
  539.8 2.5 fusion.3
  542.3 34.9 %all_gather.94 = bf16[640,768]{1,0:T(8,128)(2,1)S(1)} all-gather(bf16[80,768]{1,0:T(8,128)(2,1)S(1)} %fusion.3), channel_id=1, replica_groups=mesh['expert'=4,'group'=8] {'group'}, dimensions={0}, use_global_device_ids=true | all-gather | bytes 1105920 | tf_op jit(solution)/shard_map/all_gather | solution.py:75
  578.5 3.7 all-to-all-start.1
  582.2 37.4 %all-gather.43.cloned.1.call-done = bf16[2048,768]{1,0:T(8,128)(2,1)} async-done(((bf16[256,768]{1,0:T(8,128)(2,1)}), bf16[2048,768]{1,0:T(8,128)(2,1)}) %all-gather.43.cloned.1.call-update) | async-done | bytes 3145744 | tf_op jit(solution)/shard_map/all_gather | solution.py:64
  619.6 2.5 fusion.43
  622.1 58.5 %all-gather.47.cloned.1.call-done = bf16[2048,768]{1,0:T(8,128)(2,1)} async-done(((bf16[256,768]{1,0:T(8,128)(2,1)}), bf16[2048,768]{1,0:T(8,128)(2,1)}) %all-gather.47.cloned.1.call-update) | async-done | bytes 3145744 | tf_op jit(solution)/shard_map/all_gather | solution.py:65
  680.7 2.6 fusion.4
  683.3 34.9 %all_gather.100 = bf16[640,768]{1,0:T(8,128)(2,1)S(1)} all-gather(bf16[80,768]{1,0:T(8,128)(2,1)S(1)} %fusion.4), channel_id=1, replica_groups=mesh['expert'=4,'group'=8] {'group'}, dimensions={0}, use_global_device_ids=true | all-gather | bytes 1105920 | tf_op jit(solution)/shard_map/all_gather | solution.py:75
  718.2 1.3 fusion.15
  719.4 4.2 all-to-all-start.2
  723.6 37.4 %all-gather.53.cloned.1.call-done = bf16[2048,768]{1,0:T(8,128)(2,1)} async-done(((bf16[256,768]{1,0:T(8,128)(2,1)}), bf16[2048,768]{1,0:T(8,128)(2,1)}) %all-gather.53.cloned.1.call-update) | async-done | bytes 3145744 | tf_op jit(solution)/shard_map/all_gather | solution.py:64
  761.0 2.5 fusion.44
  763.5 58.5 %all-gather.57.cloned.1.call-done = bf16[2048,768]{1,0:T(8,128)(2,1)} async-done(((bf16[256,768]{1,0:T(8,128)(2,1)}), bf16[2048,768]{1,0:T(8,128)(2,1)}) %all-gather.57.cloned.1.call-update) | async-done | bytes 3145744 | tf_op jit(solution)/shard_map/all_gather | solution.py:65
  822.1 2.5 fusion.5
  824.6 32.8 %all_gather.106 = bf16[640,768]{1,0:T(8,128)(2,1)S(1)} all-gather(bf16[80,768]{1,0:T(8,128)(2,1)S(1)} %fusion.5), channel_id=1, replica_groups=mesh['expert'=4,'group'=8] {'group'}, dimensions={0}, use_global_device_ids=true | all-gather | bytes 1105920 | tf_op jit(solution)/shard_map/all_gather | solution.py:75
  858.6 3.5 all-to-all-start.3
  862.3 1.3 gather_fusion
  863.6 1.3 gather_fusion.2
  864.8 1.3 gather_fusion.4
  866.1 1.3 gather_fusion.6
  869.8 3.9 all-to-all-done.3
  875.8 3.8 scatter_custom_fusion
  879.6 5.7 scatter_custom_fusion.1
  885.3 5.7 scatter_custom_fusion.2
  891.0 5.9 scatter_custom_fusion.3
  896.9 3.8 convert_element_type.93
  (114 shorter events, 21.4 us)
Async XLA Ops:
  6.5 187.3 %copy-start = (bf16[512,2048]{1,0:T(8,128)(2,1)S(1)}, bf16[512,2048]{1,0:T(8,128)(2,1)}, u32[]{:S(2)}) copy-start(bf16[512,2048]{1,0:T(8,128)(2,1)} %param.7) | copy-start | bytes 6291460
  6.5 36.6 %all-gather.21.cloned.1.call-start = ((), (), s32[]{:S(2)}) async-start(), calls=%async_computation.4 | async-start | bytes 1966080 | tf_op jit(solution)/shard_map/all_gather | solution.py:14
  20.6 43.7 %all-gather.25.cloned.1.call-start = ((), (), s32[]{:S(2)}) async-start(), calls=%async_computation.6 | async-start | bytes 1966080 | tf_op jit(solution)/shard_map/all_gather | solution.py:14
  23.2 62.4 %all-gather.31.cloned.1.call-start = ((), (), s32[]{:S(2)}) async-start(), calls=%async_computation.9 | async-start | bytes 1966080 | tf_op jit(solution)/shard_map/all_gather | solution.py:14
  23.9 82.7 %all-gather.35.cloned.1.call-start = ((), (), s32[]{:S(2)}) async-start(), calls=%async_computation.11 | async-start | bytes 1966080 | tf_op jit(solution)/shard_map/all_gather | solution.py:14
  24.5 103.2 %all-gather.41.cloned.1.call-start = ((), (), s32[]{:S(2)}) async-start(), calls=%async_computation.14 | async-start | bytes 1966080 | tf_op jit(solution)/shard_map/all_gather | solution.py:14
  25.1 123.7 %all-gather.45.cloned.1.call-start = ((), (), s32[]{:S(2)}) async-start(), calls=%async_computation.16 | async-start | bytes 1966080 | tf_op jit(solution)/shard_map/all_gather | solution.py:14
  25.7 144.3 %all-gather.51.cloned.1.call-start = ((), (), s32[]{:S(2)}) async-start(), calls=%async_computation.19 | async-start | bytes 1966080 | tf_op jit(solution)/shard_map/all_gather | solution.py:14
  26.4 164.8 %all-gather.55.cloned.1.call-start = ((), (), s32[]{:S(2)}) async-start(), calls=%async_computation.21 | async-start | bytes 1966080 | tf_op jit(solution)/shard_map/all_gather | solution.py:14
  27.2 185.4 %all-gather.29.cloned.1.call-start = ((), (), s32[]{:S(2)}) async-start(), calls=%async_computation.8 | async-start | bytes 1966080 | tf_op jit(solution)/shard_map/all_gather | solution.py:14
  29.8 203.8 %all-gather.39.cloned.1.call-start = ((), (), s32[]{:S(2)}) async-start(), calls=%async_computation.13 | async-start | bytes 1966080 | tf_op jit(solution)/shard_map/all_gather | solution.py:14
  30.4 224.4 %all-gather.49.cloned.1.call-start = ((), (), s32[]{:S(2)}) async-start(), calls=%async_computation.18 | async-start | bytes 1966080 | tf_op jit(solution)/shard_map/all_gather | solution.py:14
  31.1 244.8 %all-gather.59.cloned.1.call-start = ((), (), s32[]{:S(2)}) async-start(), calls=%async_computation.23 | async-start | bytes 1966080 | tf_op jit(solution)/shard_map/all_gather | solution.py:14
  31.7 306.5 %all-gather.23.cloned.1.call-start = ((), (), s32[]{:S(2)}) async-start(), calls=%async_computation.5 | async-start | bytes 3538944 | tf_op jit(solution)/shard_map/all_gather | solution.py:64
  45.6 353.3 %all-gather.27.cloned.1.call-start = ((), (), s32[]{:S(2)}) async-start(), calls=%async_computation.7 | async-start | bytes 3538944 | tf_op jit(solution)/shard_map/all_gather | solution.py:65
  66.8 411.9 %all-gather.33.cloned.1.call-start = ((), (), s32[]{:S(2)}) async-start(), calls=%async_computation.10 | async-start | bytes 3538944 | tf_op jit(solution)/shard_map/all_gather | solution.py:64
  88.1 451.7 %all-gather.37.cloned.1.call-start = ((), (), s32[]{:S(2)}) async-start(), calls=%async_computation.12 | async-start | bytes 3538944 | tf_op jit(solution)/shard_map/all_gather | solution.py:65
  109.2 63.4 %copy-start.6 = (s32[512,8]{0,1:T(8,128)S(1)}, s32[512,8]{0,1:T(8,128)}, u32[]{:S(2)}) copy-start(s32[512,8]{0,1:T(8,128)} %param.8) | copy-start | bytes 49156
  109.2 65.4 %copy-start.7 = (f32[512,8]{0,1:T(8,128)S(1)}, f32[512,8]{0,1:T(8,128)}, u32[]{:S(2)}) copy-start(f32[512,8]{0,1:T(8,128)} %param.9) | copy-start | bytes 49156
  109.2 510.4 %all-gather.43.cloned.1.call-start = ((), (), s32[]{:S(2)}) async-start(), calls=%async_computation.15 | async-start | bytes 3538944 | tf_op jit(solution)/shard_map/all_gather | solution.py:64
  130.2 550.5 %all-gather.47.cloned.1.call-start = ((), (), s32[]{:S(2)}) async-start(), calls=%async_computation.17 | async-start | bytes 3538944 | tf_op jit(solution)/shard_map/all_gather | solution.py:65
  151.3 609.7 %all-gather.53.cloned.1.call-start = ((), (), s32[]{:S(2)}) async-start(), calls=%async_computation.20 | async-start | bytes 3538944 | tf_op jit(solution)/shard_map/all_gather | solution.py:64
  172.5 649.5 %all-gather.57.cloned.1.call-start = ((), (), s32[]{:S(2)}) async-start(), calls=%async_computation.22 | async-start | bytes 3538944 | tf_op jit(solution)/shard_map/all_gather | solution.py:65
  437.6 140.9 %all-to-all-start = ((f32[8,80,256]{2,1,0:T(8,128)}), f32[8,80,256]{2,1,0:T(8,128)S(1)}, u32[]{:S(2)}, u32[]{:S(2)}) async-start(f32[8,80,256]{2,1,0:T(8,128)} %fusion.19), calls=%async_computation | async-start | bytes 1310720 | tf_op jit(solution)/shard_map/all_to_all | solution.py:77
  481.3 96.0 %copy-start.5 = (bf16[768,256]{1,0:T(8,128)(2,1)S(1)}, bf16[768,256]{1,0:T(8,128)(2,1)}, u32[]{:S(2)}) copy-start(bf16[768,256]{1,0:T(8,128)(2,1)} %reduce_sum.235) | copy-start | bytes 1179652
  578.5 140.9 %all-to-all-start.1 = ((f32[8,80,256]{2,1,0:T(8,128)}), f32[8,80,256]{2,1,0:T(8,128)S(1)}, u32[]{:S(2)}, u32[]{:S(2)}) async-start(f32[8,80,256]{2,1,0:T(8,128)} %fusion.17), calls=%async_computation.1 | async-start | bytes 1310720 | tf_op jit(solution)/shard_map/all_to_all | solution.py:77
  680.7 37.5 %copy-start.4 = (bf16[768,256]{1,0:T(8,128)(2,1)S(1)}, bf16[768,256]{1,0:T(8,128)(2,1)}, u32[]{:S(2)}) copy-start(bf16[768,256]{1,0:T(8,128)(2,1)} %reduce_sum.241) | copy-start | bytes 1179652
  719.4 139.2 %all-to-all-start.2 = ((f32[8,80,256]{2,1,0:T(8,128)}), f32[8,80,256]{2,1,0:T(8,128)}, u32[]{:S(2)}, u32[]{:S(2)}) async-start(f32[8,80,256]{2,1,0:T(8,128)} %fusion.15), calls=%async_computation.2 | async-start | bytes 1310720 | tf_op jit(solution)/shard_map/all_to_all | solution.py:77
  858.6 15.2 %all-to-all-start.3 = ((f32[8,80,256]{2,1,0:T(8,128)}), f32[8,80,256]{2,1,0:T(8,128)S(1)}, u32[]{:S(2)}, u32[]{:S(2)}) async-start(f32[8,80,256]{2,1,0:T(8,128)} %fusion.13), calls=%async_computation.3 | async-start | bytes 1310720 | tf_op jit(solution)/shard_map/all_to_all | solution.py:77
  868.6 7.2 copy-start.3
  873.8 0.8 copy-start.2
  891.0 9.7 %copy-start.1 = (bf16[512,2048]{1,0:T(8,128)(2,1)S(1)}, bf16[512,2048]{1,0:T(8,128)(2,1)}, u32[]{:S(2)}) copy-start(bf16[512,2048]{1,0:T(8,128)(2,1)} %param.7) | copy-start | bytes 6291460
Sparse Core Ops, SparseCore 0:
  20.7 22.3 all-gather.20
  44.7 19.6 all-gather.24
  65.9 19.6 all-gather.30
  87.0 19.6 all-gather.34
  108.0 19.6 all-gather.40
  129.1 19.6 all-gather.44
  150.3 19.6 all-gather.50
  171.6 19.6 all-gather.54
  192.8 19.6 all-gather.28
  213.9 19.6 all-gather.38
  235.2 19.6 all-gather.48
  256.2 19.6 all-gather.58
  278.1 60.0 all-gather.22
  340.2 58.6 all-gather.26
  400.9 77.7 all-gather.32
  480.8 58.9 all-gather.36
  541.8 77.7 all-gather.42
  621.7 58.9 all-gather.46
  682.9 78.0 all-gather.52
  763.0 58.9 all-gather.56
